TPU v7x, 512 devices: a whole 4x8x8 slice. The times are simulated.
512 devices in a mesh: state: 64 (over y_hi, z, x), lat: 8 (over y_lo, core).
Axes of the slice: x: 4, y: 8 (y_hi: 2, y_lo: 4; y = y_hi * 4 + y_lo), z: 8, core: 2. Of those that a mesh axis runs over, the one named last changes fastest.
Arguments:
- spins: int32 [64, 8, 128], P('state', 'lat'), may hold values from -1 to 1, as said below
- embed_w: bfloat16 [64, 9], replicated, may hold values from -2 to 2
- block_w: bfloat16 [16, 1, 2, 64, 576], replicated, may hold values from -0.25 to 0.25
- readout: bfloat16 [16, 64], replicated, may hold values from -0.09375 to 0.09375
- amp_cot: float32 [16, 64], replicated, may hold values from -6 to 6
Outputs:
- log_amp: float32 [16, 64], replicated
- block_grad: float32 [1024, 1, 2, 576], P('state')
- embed_grad: float32 [64, 9], replicated
Inputs may be any that keep to these rules, and one draw needn't show every extreme that they name: `spins`: every entry is -1 or +1.
All inputs are finite; a program needn't handle non-finite values.
Results may differ from a plain program's by a relative error of at most 0.00083.
Values may be sent and summed in bfloat16 or wider, within the bound.
No kernel may reach another device: no remote copies, remote signals or barrier semaphores. Data moves between devices by JAX's collectives and lax.ppermute only.
A program may use at most 64 MiB of HBM per device.

v0:
```python
import math
import jax
import jax.numpy as jnp
from jax import lax
from jax.sharding import PartitionSpec as P


def extended(block, sides, width):
    for axis, dim in sides:
        count = lax.axis_size(axis)
        forward = [(i, i + 1) for i in range(count - 1)]
        forward.append((count - 1, 0))
        backward = [(target, source) for source, target in forward]
        low = lax.ppermute(
            lax.slice_in_dim(block, block.shape[dim] - width, None, axis=dim), axis, forward
        )
        high = lax.ppermute(lax.slice_in_dim(block, 0, width, axis=dim), axis, backward)
        block = jnp.concatenate([low, block, high], axis=dim)
    return block


def swapped(value, axis, bit):
    mask = 2**bit
    pairs = [(source, source ^ mask) for source in range(lax.axis_size(axis))]
    return lax.ppermute(value, axis, pairs)


def make_patches(padded):
    row_count = padded.shape[2] - 2
    col_count = padded.shape[3] - 2
    pieces = []
    for step_x in range(3):
        for step_y in range(3):
            pieces.append(padded[:, :, step_x : step_x + row_count, step_y : step_y + col_count])
    return jnp.concatenate(pieces, axis=1)


def conv_apply(weight, patches):
    return jnp.einsum("ok,nkxy->noxy", weight, patches, preferred_element_type=jnp.float32)


def flipped(weight):
    out_count = weight.shape[0]
    in_count = weight.shape[1] // 9
    return jnp.transpose(weight.reshape(out_count, 9, in_count)[:, ::-1, :], (2, 1, 0)).reshape(
        in_count, 9 * out_count
    )


def grad_from(inner_field, cot_patches):
    channel_count = inner_field.shape[1]
    joined = jnp.einsum(
        "nqxy,nkxy->kq", inner_field, cot_patches, preferred_element_type=jnp.float32
    )
    turned = joined.reshape(9, -1, channel_count)[::-1]
    return jnp.transpose(turned, (1, 0, 2)).reshape(turned.shape[1], 9 * channel_count)


def spin_contract(cotan, padded):
    row_count = cotan.shape[2]
    col_count = cotan.shape[3]
    offset_parts = []
    for step_x in range(3):
        for step_y in range(3):
            window = padded[:, 0, step_x : step_x + row_count, step_y : step_y + col_count].astype(
                jnp.float32
            )
            offset_parts.append(
                jnp.einsum("ncxy,nxy->c", cotan, window, precision=lax.Precision.HIGHEST)
            )
    return jnp.stack(offset_parts, axis=1)


def silu_slope(pre_act):
    sigmoid_value = jax.nn.sigmoid(pre_act)
    return sigmoid_value * (1.0 + pre_act * (1.0 - sigmoid_value))


def extend(source):
    padded = extended(source, (("lat", 2),), 1)
    return jnp.concatenate([padded[..., -1:], padded, padded[..., :1]], axis=3)


def stack_pair(payload, partner, upper_half):
    return jnp.where(
        upper_half, jnp.concatenate([partner, payload], 0), jnp.concatenate([payload, partner], 0)
    )


def split_pair(summed, upper_half):
    half_count = summed.shape[0] // 2
    lower_part = summed[:half_count]
    upper_part = summed[half_count:]
    return (
        jnp.where(upper_half, upper_part, lower_part),
        jnp.where(upper_half, lower_part, upper_part),
    )


def join_features(payload, state_index, low_bits, all_bits):
    for bit_index in range(low_bits, all_bits):
        partner = swapped(payload, "state", bit_index)
        payload = stack_pair(payload, partner, state_index >> bit_index & 1 == 1)
    return payload


def spread_cotangent(summed, state_index, low_bits, all_bits):
    for bit_index in reversed(range(low_bits, all_bits)):
        kept_part, sent_part = split_pair(summed, state_index >> bit_index & 1 == 1)
        summed = kept_part + swapped(sent_part, "state", bit_index)
    return summed


def spread_grads(summed, state_index, low_bits):
    for bit_index in reversed(range(low_bits)):
        kept_part, sent_part = split_pair(summed, state_index >> bit_index & 1 == 1)
        summed = kept_part + swapped(sent_part, "state", bit_index)
    return summed


def run_state(in_first, extend_fn, w_state, v_float, cot_vector, site_scale):
    stream = in_first[:, :, 1:-1, 1:-1].astype(jnp.float32)
    block_index = 0
    z_one = conv_apply(w_state[block_index, 0], make_patches(in_first))
    g_one = jax.nn.silu(z_one).astype(jnp.bfloat16)
    stream = stream + conv_apply(w_state[block_index, 1], make_patches(extend_fn(g_one)))
    saved_list = [(in_first[:, :, 1:-1, 1:-1], z_one, g_one)]
    part_row = (
        jnp.einsum("c,kcxy->k", v_float, jax.nn.silu(stream), precision=lax.Precision.HIGHEST)
        * site_scale
    )
    d_stream = (
        (cot_vector * site_scale)[:, None, None, None]
        * v_float[None, :, None, None]
        * silu_slope(stream)
    )
    grad_list = [None] * w_state.shape[0]
    for block_index in reversed(range(w_state.shape[0])):
        inner_field, z_one, g_one = saved_list[block_index]
        dz_two = d_stream.astype(jnp.bfloat16)
        cot_two = make_patches(extend_fn(dz_two))
        grad_two = grad_from(g_one, cot_two)
        dz_one = (conv_apply(flipped(w_state[block_index, 1]), cot_two) * silu_slope(z_one)).astype(
            jnp.bfloat16
        )
        cot_one = make_patches(extend_fn(dz_one))
        grad_one = grad_from(inner_field, cot_one)
        d_stream = d_stream + conv_apply(flipped(w_state[block_index, 0]), cot_one)
        grad_list[block_index] = jnp.stack([grad_one, grad_two])
    return (part_row, jnp.stack(grad_list), d_stream)


def local(spins, embed_w, block_w, readout, amp_cot):
    state_total = lax.axis_size("state")
    lat_count = lax.axis_size("lat")
    state_count = block_w.shape[0]
    group_count = state_total // state_count
    low_bits = group_count.bit_length() - 1
    all_bits = state_total.bit_length() - 1
    state_index = lax.axis_index("state")
    my_state = state_index // group_count
    my_group = state_index % group_count
    held_count = spins.shape[0]
    site_scale = 1.0 / math.sqrt(spins.shape[1] * lat_count * spins.shape[2])
    w_state = lax.dynamic_index_in_dim(block_w, my_state, 0, keepdims=False)
    v_float = lax.dynamic_index_in_dim(readout, my_state, 0, keepdims=False).astype(jnp.float32)
    cot_row = lax.dynamic_index_in_dim(amp_cot, my_state, 0, keepdims=False).reshape(
        state_count, group_count, held_count
    )
    group_pick = (jnp.arange(group_count) == my_group).astype(jnp.float32)
    group_cot = jnp.sum(cot_row * group_pick[None, :, None], axis=1).reshape(
        state_count * held_count
    )
    spin_field = spins.astype(jnp.bfloat16)[:, None]
    spin_pad = extend(spin_field)
    h_zero = conv_apply(embed_w, make_patches(spin_pad)).astype(jnp.bfloat16)
    h_pad = extend(h_zero)
    in_first = join_features(h_pad, state_index, low_bits, all_bits)
    group_row, grad_stack, d_stream = run_state(
        in_first, extend, w_state, v_float, group_cot, site_scale
    )
    own_cot_field = spread_cotangent(d_stream, state_index, low_bits, all_bits)
    contrib = spin_contract(own_cot_field, spin_pad)
    state_pick = (jnp.arange(state_count) == my_state).astype(jnp.float32)
    spread_row = (
        group_row.reshape(state_count, 1, held_count) * group_pick[None, :, None]
    ).reshape(-1)
    amp_part = state_pick[:, None] * spread_row[None, :]
    log_amp, embed_grad = lax.psum((amp_part, contrib), ("state", "lat"))
    by_channel = jnp.transpose(grad_stack, (2, 0, 1, 3))
    own_rows = spread_grads(by_channel, state_index, low_bits)
    block_grad = lax.psum(own_rows, "lat")
    return (log_amp, block_grad, embed_grad)


def solution(mesh):
    return jax.shard_map(
        local,
        mesh=mesh,
        in_specs=(P("state", "lat", None), P(), P(), P(), P()),
        out_specs=(P(), P("state", None, None, None), P()),
        check_vma=False,
    )
```

profile of v0, /device:TPU:1, one launch (start us, length us, event | category | flops | bytes accessed | tf_op | source)
XLA Modules:
  0.0 407.7 jit_solution(13275533866061689292)
XLA Ops:
  8.0 8.8 %collective-permute-start.1 = (bf16[1,1,1,128]{3,2,1,0:T(2,128)(2,1)S(1)}, bf16[1,1,1,128]{3,2,1,0:T(2,128)(2,1)S(1)}, u32[]{:S(2)}, u32[]{:S(2)}) collective-permute-start(bf16[1,1,1,128]{3,2,1,0:T(2,128)(2,1)S(1)} %convert_bitcast_fusion), channel_id=1, source_target_pairs={{1,0},{2,1},{3,2},{4,3},{5,4},{6,5},{7,6},{0,7},{9,8},{10,9},{11,1... | collective-permute-start | bytes 776 | tf_op jit(solution)/shard_map/ppermute | solution.py:17
  16.8 1.9 collective-permute-start
  25.2 5.6 %collective-permute-start.3 = (bf16[1,64,1,128]{3,1,2,0:T(8,128)(2,1)S(1)}, bf16[1,64,1,128]{3,1,2,0:T(8,128)(2,1)S(1)}, u32[]{:S(2)}, u32[]{:S(2)}) collective-permute-start(bf16[1,64,1,128]{3,1,2,0:T(8,128)(2,1)S(1)} %fusion.29), channel_id=1, source_target_pairs={{1,0},{2,1},{3,2},{4,3},{5,4},{6,5},{7,6},{0,7},{9,8},{10,9},{11,1... | collective-permute-start | bytes 49160 | tf_op jit(solution)/shard_map/ppermute | solution.py:17
  30.8 1.9 collective-permute-start.2
  32.8 1.1 collective-permute-done.2
  34.1 1.9 collective-permute-start.4
  36.0 3.4 collective-permute-done.4
  39.6 4.1 %collective-permute-start.5 = (bf16[2,64,3,130]{3,1,2,0:T(8,128)(2,1)S(1)}, bf16[2,64,3,130]{3,1,2,0:T(8,128)(2,1)S(1)}, u32[]{:S(2)}, u32[]{:S(2)}) collective-permute-start(bf16[2,64,3,130]{3,1,2,0:T(8,128)(2,1)S(1)} %maximum_select_fusion.3), channel_id=1, source_target_pairs={{0,64},{8,72},{16,80},{24,88},{32,96},{40,104},{48,112},{56,120},{... | collective-permute-start | bytes 299528 | tf_op jit(solution)/shard_map/ppermute | solution.py:25
  44.5 4.5 %collective-permute-done.5 = bf16[2,64,3,130]{3,1,2,0:T(8,128)(2,1)S(1)} collective-permute-done((bf16[2,64,3,130]{3,1,2,0:T(8,128)(2,1)S(1)}, bf16[2,64,3,130]{3,1,2,0:T(8,128)(2,1)S(1)}, u32[]{:S(2)}, u32[]{:S(2)}) %collective-permute-start.5) | collective-permute-done | bytes 99872 | tf_op jit(solution)/shard_map/ppermute | solution.py:25
  49.2 8.3 %collective-permute-start.6 = (bf16[4,64,3,130]{3,1,2,0:T(8,128)(2,1)S(1)}, bf16[4,64,3,130]{3,1,2,0:T(8,128)(2,1)S(1)}, u32[]{:S(2)}, u32[]{:S(2)}) collective-permute-start(bf16[4,64,3,130]{3,1,2,0:T(8,128)(2,1)S(1)} %maximum_select_fusion.2), channel_id=1, source_target_pairs={{0,128},{8,136},{16,144},{24,152},{32,160},{40,168},{48,176},{56,1... | collective-permute-start | bytes 599048 | tf_op jit(solution)/shard_map/ppermute | solution.py:25
  58.0 7.0 %collective-permute-done.6 = bf16[4,64,3,130]{3,1,2,0:T(8,128)(2,1)S(1)} collective-permute-done((bf16[4,64,3,130]{3,1,2,0:T(8,128)(2,1)S(1)}, bf16[4,64,3,130]{3,1,2,0:T(8,128)(2,1)S(1)}, u32[]{:S(2)}, u32[]{:S(2)}) %collective-permute-start.6) | collective-permute-done | bytes 199712 | tf_op jit(solution)/shard_map/ppermute | solution.py:25
  65.3 4.8 %collective-permute-start.7 = (bf16[8,64,3,130]{3,1,2,0:T(8,128)(2,1)S(1)}, bf16[8,64,3,130]{3,1,2,0:T(8,128)(2,1)}, u32[]{:S(2)}, u32[]{:S(2)}) collective-permute-start(bf16[8,64,3,130]{3,1,2,0:T(8,128)(2,1)S(1)} %maximum_select_fusion.1), channel_id=1, source_target_pairs={{0,256},{8,264},{16,272},{24,280},{32,288},{40,296},{48,304},{56,3... | collective-permute-start | bytes 1198088 | tf_op jit(solution)/shard_map/ppermute | solution.py:25
  71.3 11.7 %collective-permute-done.7 = bf16[8,64,3,130]{3,1,2,0:T(8,128)(2,1)} collective-permute-done((bf16[8,64,3,130]{3,1,2,0:T(8,128)(2,1)S(1)}, bf16[8,64,3,130]{3,1,2,0:T(8,128)(2,1)}, u32[]{:S(2)}, u32[]{:S(2)}) %collective-permute-start.7) | collective-permute-done | bytes 399392 | tf_op jit(solution)/shard_map/ppermute | solution.py:25
  83.0 1.9 maximum_select_fusion
  86.5 1.4 multiply_convert_fusion
  87.9 10.2 %collective-permute-start.9 = (bf16[16,64,1,128]{3,1,2,0:T(8,128)(2,1)S(1)}, bf16[16,64,1,128]{3,1,2,0:T(8,128)(2,1)S(1)}, u32[]{:S(2)}, u32[]{:S(2)}) collective-permute-start(bf16[16,64,1,128]{3,1,2,0:T(8,128)(2,1)S(1)} %get-tuple-element.37), channel_id=1, source_target_pairs={{1,0},{2,1},{3,2},{4,3},{5,4},{6,5},{7,6},{0,7},{9,8},{10,9},{11,1... | collective-permute-start | bytes 786440 | tf_op jit(solution)/shard_map/ppermute | solution.py:17
  98.1 23.5 %collective-permute-start.8 = (bf16[16,64,1,128]{3,1,2,0:T(8,128)(2,1)S(1)}, bf16[16,64,1,128]{3,1,2,0:T(8,128)(2,1)S(1)}, u32[]{:S(2)}, u32[]{:S(2)}) collective-permute-start(bf16[16,64,1,128]{3,1,2,0:T(8,128)(2,1)S(1)} %get-tuple-element.37), channel_id=1, source_target_pairs={{0,1},{1,2},{2,3},{3,4},{4,5},{5,6},{6,7},{7,0},{8,9},{9,10},{10,1... | collective-permute-start | bytes 786440 | tf_op jit(solution)/shard_map/ppermute | solution.py:14
  121.6 1.2 bitcast_convert_fusion
  127.8 3.1 fusion.67
  130.9 5.1 %collective-permute-start.11 = (bf16[16,64,1,128]{3,1,2,0:T(8,128)(2,1)S(1)}, bf16[16,64,1,128]{3,1,2,0:T(8,128)(2,1)S(1)}, u32[]{:S(2)}, u32[]{:S(2)}) collective-permute-start(bf16[16,64,1,128]{3,1,2,0:T(8,128)(2,1)S(1)} %get-tuple-element.23), channel_id=1, source_target_pairs={{1,0},{2,1},{3,2},{4,3},{5,4},{6,5},{7,6},{0,7},{9,8},{10,9},{11,1... | collective-permute-start | bytes 786440 | tf_op jit(solution)/shard_map/ppermute | solution.py:17
  136.0 1.9 collective-permute-start.10
  139.8 1.7 copy.24
  143.2 1.7 copy.33
  148.9 1.2 maximum_dynamic-update-slice_fusion.6
  152.5 2.4 collective-permute-start.13
  154.9 3.3 collective-permute-start.12
  159.7 1.8 copy.27
  161.6 2.5 collective-permute-done.12
  167.6 1.2 maximum_dynamic-update-slice_fusion.2
  170.0 2.3 convolution_bitcast_fusion.1
  174.5 4.6 %collective-permute-start.14 = (f32[32,1,2,576]{3,0,2,1:T(8,128)}, f32[32,1,2,576]{3,0,2,1:T(8,128)S(1)}, u32[]{:S(2)}, u32[]{:S(2)}) collective-permute-start(f32[32,1,2,576]{3,0,2,1:T(8,128)} %copy.28), channel_id=1, source_target_pairs={{0,16},{8,24},{16,0},{24,8},{32,48},{40,56},{48,32},{56,40},{64,80... | collective-permute-start | bytes 442376 | tf_op jit(solution)/shard_map/ppermute | solution.py:25
  179.2 2.6 fusion.20
  182.5 7.1 %collective-permute-start.16 = (f32[8,64,1,128]{3,1,2,0:T(8,128)S(1)}, f32[8,64,1,128]{3,1,2,0:T(8,128)}, u32[]{:S(2)}, u32[]{:S(2)}) collective-permute-start(f32[8,64,1,128]{3,1,2,0:T(8,128)S(1)} %slice_select_fusion.2), channel_id=1, source_target_pairs={{0,256},{8,264},{16,272},{24,280},{32,288},{40,296},{48,304},{56,3... | collective-permute-start | bytes 786440 | tf_op jit(solution)/shard_map/ppermute | solution.py:25
  190.7 1.7 select_add_fusion.1
  193.4 1.3 copy.30
  194.7 2.2 collective-permute-start.15
  196.9 4.2 %collective-permute-done.16 = f32[8,64,1,128]{3,1,2,0:T(8,128)} collective-permute-done((f32[8,64,1,128]{3,1,2,0:T(8,128)S(1)}, f32[8,64,1,128]{3,1,2,0:T(8,128)}, u32[]{:S(2)}, u32[]{:S(2)}) %collective-permute-start.16) | collective-permute-done | bytes 262176 | tf_op jit(solution)/shard_map/ppermute | solution.py:25
  201.1 1.1 select_add_fusion.2
  202.9 6.2 %collective-permute-start.17 = (f32[4,64,1,128]{3,1,2,0:T(8,128)}, f32[4,64,1,128]{3,1,2,0:T(8,128)}, u32[]{:S(2)}, u32[]{:S(2)}) collective-permute-start(f32[4,64,1,128]{3,1,2,0:T(8,128)} %slice_select_fusion.3), channel_id=1, source_target_pairs={{0,128},{8,136},{16,144},{24,152},{32,160},{40,168},{48,176},{56,1... | collective-permute-start | bytes 393224 | tf_op jit(solution)/shard_map/ppermute | solution.py:25
  210.7 1.3 mul.119
  212.0 1.2 mul.122
  213.2 1.9 copy.31
  216.8 5.6 %collective-permute-start.18 = (f32[2,64,1,128]{3,1,2,0:T(8,128)S(1)}, f32[2,64,1,128]{3,1,2,0:T(8,128)S(1)}, u32[]{:S(2)}, u32[]{:S(2)}) collective-permute-start(f32[2,64,1,128]{3,1,2,0:T(8,128)S(1)} %slice_select_fusion.4), channel_id=1, source_target_pairs={{0,64},{8,72},{16,80},{24,88},{32,96},{40,104},{48,112},{56,120},{... | collective-permute-start | bytes 196616 | tf_op jit(solution)/shard_map/ppermute | solution.py:25
  222.4 2.1 select_add_fusion
  224.6 1.9 collective-permute-start.19
  226.6 69.0 %all-reduce.3.cloned.1.call-done = f32[16,1,2,576]{0,3,2,1:T(8,128)} async-done(((f32[16,1,2,576]{0,3,2,1:T(8,128)}), f32[16,1,2,576]{0,3,2,1:T(8,128)}) %all-reduce.3.cloned.1.call-update) | async-done | bytes 73744 | tf_op jit(solution)/shard_map/psum | solution.py:192
  295.7 1.9 copy.35
  299.1 101.8 %all-reduce = (f32[16,64]{1,0:T(8,128)}, f32[64,9]{0,1:T(8,128)}) all-reduce(f32[16,64]{1,0:T(8,128)S(1)} %broadcast_multiply_fusion.1, f32[64,9]{0,1:T(8,128)S(1)} %stack.47), channel_id=1, replica_groups=mesh['state'=64,'lat'=8] {'state','lat'}, use_global_device_ids=true, to_apply=%region_1.2 | all-reduce | flops 1600 | bytes 12800 | tf_op jit(solution)/shard_map/psum | solution.py:189
  (177 shorter events, 43.4 us)
Async XLA Ops:
  7.2 63.4 %copy-start = (bf16[16,1,2,64,576]{4,3,2,1,0:T(8,128)(2,1)S(1)}, bf16[16,1,2,64,576]{4,3,2,1,0:T(8,128)(2,1)}, u32[]{:S(2)}) copy-start(bf16[16,1,2,64,576]{4,3,2,1,0:T(8,128)(2,1)} %param.7) | copy-start | bytes 7077892
  7.2 288.5 %all-reduce.3.cloned.1.call-start = ((), (), s32[]{:S(2)}) async-start(), calls=%async_computation | async-start | bytes 1179648 | tf_op jit(solution)/shard_map/psum | solution.py:192
  8.0 10.7 %collective-permute-start.1 = (bf16[1,1,1,128]{3,2,1,0:T(2,128)(2,1)S(1)}, bf16[1,1,1,128]{3,2,1,0:T(2,128)(2,1)S(1)}, u32[]{:S(2)}, u32[]{:S(2)}) collective-permute-start(bf16[1,1,1,128]{3,2,1,0:T(2,128)(2,1)S(1)} %convert_bitcast_fusion), channel_id=1, source_target_pairs={{1,0},{2,1},{3,2},{4,3},{5,4},{6,5},{7,6},{0,7},{9,8},{10,9},{11,1... | collective-permute-start | bytes 776 | tf_op jit(solution)/shard_map/ppermute | solution.py:17
  16.8 3.0 collective-permute-start
  18.8 14.0 %copy-start.11 = (bf16[1,1,1,128]{3,2,1,0:T(2,128)(2,1)}, bf16[1,1,1,128]{3,2,1,0:T(2,128)(2,1)S(1)}, u32[]{:S(2)}) copy-start(bf16[1,1,1,128]{3,2,1,0:T(2,128)(2,1)S(1)} %collective-permute-done.1) | copy-start | bytes 772
  19.8 12.9 %copy-start.13 = (bf16[1,1,1,128]{3,2,1,0:T(2,128)(2,1)}, bf16[1,1,1,128]{3,2,1,0:T(2,128)(2,1)S(1)}, u32[]{:S(2)}) copy-start(bf16[1,1,1,128]{3,2,1,0:T(2,128)(2,1)S(1)} %collective-permute-done) | copy-start | bytes 772
  25.2 7.5 %collective-permute-start.3 = (bf16[1,64,1,128]{3,1,2,0:T(8,128)(2,1)S(1)}, bf16[1,64,1,128]{3,1,2,0:T(8,128)(2,1)S(1)}, u32[]{:S(2)}, u32[]{:S(2)}) collective-permute-start(bf16[1,64,1,128]{3,1,2,0:T(8,128)(2,1)S(1)} %fusion.29), channel_id=1, source_target_pairs={{1,0},{2,1},{3,2},{4,3},{5,4},{6,5},{7,6},{0,7},{9,8},{10,9},{11,1... | collective-permute-start | bytes 49160 | tf_op jit(solution)/shard_map/ppermute | solution.py:17
  30.8 3.1 collective-permute-start.2
  34.1 5.4 %collective-permute-start.4 = (bf16[1,64,3,130]{3,1,2,0:T(8,128)(2,1)S(1)}, bf16[1,64,3,130]{3,1,2,0:T(8,128)(2,1)S(1)}, u32[]{:S(2)}, u32[]{:S(2)}) collective-permute-start(bf16[1,64,3,130]{3,1,2,0:T(8,128)(2,1)S(1)} %pad_maximum_fusion.21), channel_id=1, source_target_pairs={{0,32},{8,40},{16,48},{24,56},{32,0},{40,8},{48,16},{56,24},{64,96... | collective-permute-start | bytes 149768 | tf_op jit(solution)/shard_map/ppermute | solution.py:25
  39.6 9.4 %collective-permute-start.5 = (bf16[2,64,3,130]{3,1,2,0:T(8,128)(2,1)S(1)}, bf16[2,64,3,130]{3,1,2,0:T(8,128)(2,1)S(1)}, u32[]{:S(2)}, u32[]{:S(2)}) collective-permute-start(bf16[2,64,3,130]{3,1,2,0:T(8,128)(2,1)S(1)} %maximum_select_fusion.3), channel_id=1, source_target_pairs={{0,64},{8,72},{16,80},{24,88},{32,96},{40,104},{48,112},{56,120},{... | collective-permute-start | bytes 299528 | tf_op jit(solution)/shard_map/ppermute | solution.py:25
  49.2 15.8 %collective-permute-start.6 = (bf16[4,64,3,130]{3,1,2,0:T(8,128)(2,1)S(1)}, bf16[4,64,3,130]{3,1,2,0:T(8,128)(2,1)S(1)}, u32[]{:S(2)}, u32[]{:S(2)}) collective-permute-start(bf16[4,64,3,130]{3,1,2,0:T(8,128)(2,1)S(1)} %maximum_select_fusion.2), channel_id=1, source_target_pairs={{0,128},{8,136},{16,144},{24,152},{32,160},{40,168},{48,176},{56,1... | collective-permute-start | bytes 599048 | tf_op jit(solution)/shard_map/ppermute | solution.py:25
  65.3 17.7 %collective-permute-start.7 = (bf16[8,64,3,130]{3,1,2,0:T(8,128)(2,1)S(1)}, bf16[8,64,3,130]{3,1,2,0:T(8,128)(2,1)}, u32[]{:S(2)}, u32[]{:S(2)}) collective-permute-start(bf16[8,64,3,130]{3,1,2,0:T(8,128)(2,1)S(1)} %maximum_select_fusion.1), channel_id=1, source_target_pairs={{0,256},{8,264},{16,272},{24,280},{32,288},{40,296},{48,304},{56,3... | collective-permute-start | bytes 1198088 | tf_op jit(solution)/shard_map/ppermute | solution.py:25
  70.6 15.9 %copy-start.7 = (bf16[1,2,64,576]{3,2,1,0:T(8,128)(2,1)}, bf16[1,2,64,576]{3,2,1,0:T(8,128)(2,1)S(1)}, u32[]{:S(2)}) copy-start(bf16[1,2,64,576]{3,2,1,0:T(8,128)(2,1)S(1)} %dynamic-slice_bitcast_fusion) | copy-start | bytes 442372
  84.9 1.5 copy-start.2
  87.9 36.7 %collective-permute-start.9 = (bf16[16,64,1,128]{3,1,2,0:T(8,128)(2,1)S(1)}, bf16[16,64,1,128]{3,1,2,0:T(8,128)(2,1)S(1)}, u32[]{:S(2)}, u32[]{:S(2)}) collective-permute-start(bf16[16,64,1,128]{3,1,2,0:T(8,128)(2,1)S(1)} %get-tuple-element.37), channel_id=1, source_target_pairs={{1,0},{2,1},{3,2},{4,3},{5,4},{6,5},{7,6},{0,7},{9,8},{10,9},{11,1... | collective-permute-start | bytes 786440 | tf_op jit(solution)/shard_map/ppermute | solution.py:17
  98.1 27.3 %collective-permute-start.8 = (bf16[16,64,1,128]{3,1,2,0:T(8,128)(2,1)S(1)}, bf16[16,64,1,128]{3,1,2,0:T(8,128)(2,1)S(1)}, u32[]{:S(2)}, u32[]{:S(2)}) collective-permute-start(bf16[16,64,1,128]{3,1,2,0:T(8,128)(2,1)S(1)} %get-tuple-element.37), channel_id=1, source_target_pairs={{0,1},{1,2},{2,3},{3,4},{4,5},{5,6},{6,7},{7,0},{8,9},{9,10},{10,1... | collective-permute-start | bytes 786440 | tf_op jit(solution)/shard_map/ppermute | solution.py:14
  124.6 2.8 copy-start.16
  126.9 0.9 copy-start.8
  130.9 14.5 %collective-permute-start.11 = (bf16[16,64,1,128]{3,1,2,0:T(8,128)(2,1)S(1)}, bf16[16,64,1,128]{3,1,2,0:T(8,128)(2,1)S(1)}, u32[]{:S(2)}, u32[]{:S(2)}) collective-permute-start(bf16[16,64,1,128]{3,1,2,0:T(8,128)(2,1)S(1)} %get-tuple-element.23), channel_id=1, source_target_pairs={{1,0},{2,1},{3,2},{4,3},{5,4},{6,5},{7,6},{0,7},{9,8},{10,9},{11,1... | collective-permute-start | bytes 786440 | tf_op jit(solution)/shard_map/ppermute | solution.py:17
  136.0 9.4 %collective-permute-start.10 = (bf16[16,64,1,128]{3,1,2,0:T(8,128)(2,1)S(1)}, bf16[16,64,1,128]{3,1,2,0:T(8,128)(2,1)}, u32[]{:S(2)}, u32[]{:S(2)}) collective-permute-start(bf16[16,64,1,128]{3,1,2,0:T(8,128)(2,1)S(1)} %get-tuple-element.23), channel_id=1, source_target_pairs={{0,1},{1,2},{2,3},{3,4},{4,5},{5,6},{6,7},{7,0},{8,9},{9,10},{10,1... | collective-permute-start | bytes 786440 | tf_op jit(solution)/shard_map/ppermute | solution.py:14
  150.7 0.9 copy-start.10
  150.7 1.1 copy-start.28
  152.5 9.1 %collective-permute-start.13 = (bf16[16,64,1,128]{3,1,2,0:T(8,128)(2,1)S(1)}, bf16[16,64,1,128]{3,1,2,0:T(8,128)(2,1)S(1)}, u32[]{:S(2)}, u32[]{:S(2)}) collective-permute-start(bf16[16,64,1,128]{3,1,2,0:T(8,128)(2,1)S(1)} %fusion.26), channel_id=1, source_target_pairs={{1,0},{2,1},{3,2},{4,3},{5,4},{6,5},{7,6},{0,7},{9,8},{10,9},{11,1... | collective-permute-start | bytes 786440 | tf_op jit(solution)/shard_map/ppermute | solution.py:17
  154.9 9.2 %collective-permute-start.12 = (bf16[16,64,1,128]{3,1,2,0:T(8,128)(2,1)S(1)}, bf16[16,64,1,128]{3,1,2,0:T(8,128)(2,1)}, u32[]{:S(2)}, u32[]{:S(2)}) collective-permute-start(bf16[16,64,1,128]{3,1,2,0:T(8,128)(2,1)S(1)} %fusion.26), channel_id=1, source_target_pairs={{0,1},{1,2},{2,3},{3,4},{4,5},{5,6},{6,7},{7,0},{8,9},{9,10},{10,1... | collective-permute-start | bytes 786440 | tf_op jit(solution)/shard_map/ppermute | solution.py:14
  170.0 2.3 copy-start.15
  170.0 2.5 copy-start.6
  172.3 6.8 %copy-start.17 = (f32[16,64]{1,0:T(8,128)S(1)}, f32[16,64]{1,0:T(8,128)}, u32[]{:S(2)}) copy-start(f32[16,64]{1,0:T(8,128)} %copy-done.16) | copy-start | bytes 12292
  172.6 0.8 copy-start.1
  173.4 5.8 %copy-start.9 = (bf16[64,9,64]{0,2,1:T(8,128)(2,1)S(1)}, bf16[64,9,64]{0,2,1:T(8,128)(2,1)}, u32[]{:S(2)}) copy-start(bf16[64,9,64]{0,2,1:T(8,128)(2,1)} %copy.33) | copy-start | bytes 221188
  174.5 15.2 %collective-permute-start.14 = (f32[32,1,2,576]{3,0,2,1:T(8,128)}, f32[32,1,2,576]{3,0,2,1:T(8,128)S(1)}, u32[]{:S(2)}, u32[]{:S(2)}) collective-permute-start(f32[32,1,2,576]{3,0,2,1:T(8,128)} %copy.28), channel_id=1, source_target_pairs={{0,16},{8,24},{16,0},{24,8},{32,48},{40,56},{48,32},{56,40},{64,80... | collective-permute-start | bytes 442376 | tf_op jit(solution)/shard_map/ppermute | solution.py:25
  181.7 0.8 copy-start.3
  182.5 18.6 %collective-permute-start.16 = (f32[8,64,1,128]{3,1,2,0:T(8,128)S(1)}, f32[8,64,1,128]{3,1,2,0:T(8,128)}, u32[]{:S(2)}, u32[]{:S(2)}) collective-permute-start(f32[8,64,1,128]{3,1,2,0:T(8,128)S(1)} %slice_select_fusion.2), channel_id=1, source_target_pairs={{0,256},{8,264},{16,272},{24,280},{32,288},{40,296},{48,304},{56,3... | collective-permute-start | bytes 786440 | tf_op jit(solution)/shard_map/ppermute | solution.py:25
  194.7 18.5 %collective-permute-start.15 = (f32[16,1,2,576]{3,0,2,1:T(8,128)S(1)}, f32[16,1,2,576]{3,0,2,1:T(8,128)}, u32[]{:S(2)}, u32[]{:S(2)}) collective-permute-start(f32[16,1,2,576]{3,0,2,1:T(8,128)S(1)} %copy.30), channel_id=1, source_target_pairs={{0,8},{8,0},{16,24},{24,16},{32,40},{40,32},{48,56},{56,48},{64,72... | collective-permute-start | bytes 221192 | tf_op jit(solution)/shard_map/ppermute | solution.py:25
  202.9 12.2 %collective-permute-start.17 = (f32[4,64,1,128]{3,1,2,0:T(8,128)}, f32[4,64,1,128]{3,1,2,0:T(8,128)}, u32[]{:S(2)}, u32[]{:S(2)}) collective-permute-start(f32[4,64,1,128]{3,1,2,0:T(8,128)} %slice_select_fusion.3), channel_id=1, source_target_pairs={{0,128},{8,136},{16,144},{24,152},{32,160},{40,168},{48,176},{56,1... | collective-permute-start | bytes 393224 | tf_op jit(solution)/shard_map/ppermute | solution.py:25
  213.2 13.4 %copy-start.26 = (f32[16]{0:T(128)S(1)}, f32[16]{0:T(128)}, u32[]{:S(2)}) copy-start(f32[16]{0:T(128)} %compare_convert_fusion.1) | copy-start | bytes 196
  213.2 13.4 %copy-start.27 = (f32[64]{0:T(128)S(1)}, f32[64]{0:T(128)}, u32[]{:S(2)}) copy-start(f32[64]{0:T(128)} %mul.122) | copy-start | bytes 772
  215.2 82.4 %copy-start.25 = (s32[1,1,128]{2,1,0:T(1,128)S(1)}, s32[1,1,128]{2,1,0:T(1,128)}, u32[]{:S(2)}) copy-start(s32[1,1,128]{2,1,0:T(1,128)} %param.5) | copy-start | bytes 1540
  215.2 82.5 %copy-start.19 = (bf16[1,1,1,128]{3,2,1,0:T(2,128)(2,1)S(1)}, bf16[1,1,1,128]{3,2,1,0:T(2,128)(2,1)}, u32[]{:S(2)}) copy-start(bf16[1,1,1,128]{3,2,1,0:T(2,128)(2,1)} %get-tuple-element.20) | copy-start | bytes 772
  215.2 82.7 %copy-start.20 = (bf16[1,1,1,128]{3,2,1,0:T(2,128)(2,1)S(1)}, bf16[1,1,1,128]{3,2,1,0:T(2,128)(2,1)}, u32[]{:S(2)}) copy-start(bf16[1,1,1,128]{3,2,1,0:T(2,128)(2,1)} %get-tuple-element.18) | copy-start | bytes 772
  215.2 82.9 %copy-start.21 = (bf16[1,1,1,128]{3,2,1,0:T(2,128)(2,1)S(1)}, bf16[1,1,1,128]{3,2,1,0:T(2,128)(2,1)}, u32[]{:S(2)}) copy-start(bf16[1,1,1,128]{3,2,1,0:T(2,128)(2,1)} %get-tuple-element.16) | copy-start | bytes 772
  216.8 81.4 %copy-start.22 = (bf16[1,1,1,128]{3,2,1,0:T(2,128)(2,1)S(1)}, bf16[1,1,1,128]{3,2,1,0:T(2,128)(2,1)}, u32[]{:S(2)}) copy-start(bf16[1,1,1,128]{3,2,1,0:T(2,128)(2,1)} %get-tuple-element.14) | copy-start | bytes 772
  216.8 81.6 %copy-start.23 = (bf16[1,1,1,128]{3,2,1,0:T(2,128)(2,1)S(1)}, bf16[1,1,1,128]{3,2,1,0:T(2,128)(2,1)}, u32[]{:S(2)}) copy-start(bf16[1,1,1,128]{3,2,1,0:T(2,128)(2,1)} %get-tuple-element.12) | copy-start | bytes 772
  216.8 81.7 %copy-start.18 = (bf16[1,1,1,128]{3,2,1,0:T(2,128)(2,1)S(1)}, bf16[1,1,1,128]{3,2,1,0:T(2,128)(2,1)}, u32[]{:S(2)}) copy-start(bf16[1,1,1,128]{3,2,1,0:T(2,128)(2,1)} %get-tuple-element.22) | copy-start | bytes 772
  216.8 81.9 %copy-start.14 = (bf16[1,1,1,128]{3,2,1,0:T(2,128)(2,1)S(1)}, bf16[1,1,1,128]{3,2,1,0:T(2,128)(2,1)}, u32[]{:S(2)}) copy-start(bf16[1,1,1,128]{3,2,1,0:T(2,128)(2,1)} %copy-done.13) | copy-start | bytes 772
  216.8 82.0 %copy-start.12 = (bf16[1,1,1,128]{3,2,1,0:T(2,128)(2,1)S(1)}, bf16[1,1,1,128]{3,2,1,0:T(2,128)(2,1)}, u32[]{:S(2)}) copy-start(bf16[1,1,1,128]{3,2,1,0:T(2,128)(2,1)} %copy-done.11) | copy-start | bytes 772
  216.8 7.8 %copy-start.5 = (f32[4,64,1,128]{3,1,2,0:T(8,128)S(1)}, f32[4,64,1,128]{3,1,2,0:T(8,128)}, u32[]{:S(2)}) copy-start(f32[4,64,1,128]{3,1,2,0:T(8,128)} %copy-done.4) | copy-start | bytes 393220
  216.8 7.7 %collective-permute-start.18 = (f32[2,64,1,128]{3,1,2,0:T(8,128)S(1)}, f32[2,64,1,128]{3,1,2,0:T(8,128)S(1)}, u32[]{:S(2)}, u32[]{:S(2)}) collective-permute-start(f32[2,64,1,128]{3,1,2,0:T(8,128)S(1)} %slice_select_fusion.4), channel_id=1, source_target_pairs={{0,64},{8,72},{16,80},{24,88},{32,96},{40,104},{48,112},{56,120},{... | collective-permute-start | bytes 196616 | tf_op jit(solution)/shard_map/ppermute | solution.py:25
  224.6 72.9 %collective-permute-start.19 = (f32[1,64,1,128]{3,1,2,0:T(8,128)S(1)}, f32[1,64,1,128]{3,1,2,0:T(8,128)S(1)}, u32[]{:S(2)}, u32[]{:S(2)}) collective-permute-start(f32[1,64,1,128]{3,1,2,0:T(8,128)S(1)} %slice_select_fusion.5), channel_id=1, source_target_pairs={{0,32},{8,40},{16,48},{24,56},{32,0},{40,8},{48,16},{56,24},{64,96... | collective-permute-start | bytes 98312 | tf_op jit(solution)/shard_map/ppermute | solution.py:25
  (2 other events, 1.2 us)
Sparse Core Ops, SparseCore 0:
  224.7 70.9 all-reduce.2
where the time goes:
time: 409 us; the launch traced here: 408 us
  starting transfers between devices  111 us (27%)
  waiting for transfers between devices  105 us (26%)
  blocking collectives  102 us (25%)
  other arithmetic  30.2 us (7%)
  local copies, waits for them, and re-layouts  30 us (7%)
  between operations  15 us (4%)
  matrix products  13.8 us (3%)
    psum x1, blocking collectives, local(): log_amp, embed_grad = lax.psum((amp_part, contrib), ('state', 'lat'))  102 us
    psum x1, waiting for transfers between devices, local(): block_grad = lax.psum(own_rows, 'lat')  69 us
    ppermute x10, starting transfers between devices, swapped(): return lax.ppermute(value, axis, pairs)  46.8 us
    ppermute x5, starting transfers between devices, extended(): lax.ppermute(lax.slice_in_dim(block, block.shape[dim] - width, None, axis...  32.6 us
    ppermute x5, starting transfers between devices, extended(): lax.ppermute(lax.slice_in_dim(block, 0, width, axis=dim), axis, backward)  32 us
    ppermute x10, waiting for transfers between devices, swapped(): return lax.ppermute(value, axis, pairs)  30.8 us
    unnamed x21, other arithmetic  10.9 us
    unnamed x78, local copies, waits for them, and re-layouts  9.08 us
  transfers between devices with their start and end apart: 21, of which 10 were waited for; matrix products, arithmetic and copies ran while one was open for 9% of the time, Pallas kernels for 0%

commit v1 on v0

--- a/solution.py
+++ b/solution.py
@@ -189,7 +189,7 @@
     log_amp, embed_grad = lax.psum((amp_part, contrib), ("state", "lat"))
     by_channel = jnp.transpose(grad_stack, (2, 0, 1, 3))
     own_rows = spread_grads(by_channel, state_index, low_bits)
-    block_grad = lax.psum(own_rows, "lat")
+    block_grad = jnp.sum(lax.all_gather(own_rows, "lat"), axis=0)
     return (log_amp, block_grad, embed_grad)
 
 

time: 409 us -> 333 us (0.81)
  waiting for transfers between devices: 105 us -> 63.5 us
  between operations: 15 us -> 1.63 us
  local copies, waits for them, and re-layouts: 30 us -> 18.6 us
  blocking collectives: 102 us -> 113 us
  starting transfers between devices: 111 us -> 101 us
  other arithmetic: 30.2 us -> 21.6 us
    psum x1 -> x0, waiting for transfers between devices: 69 us -> none  [local(): block_grad = lax.psum(own_rows, 'lat')]
    ppermute x5, starting transfers between devices: 32.6 us -> 11 us  [extended(): lax.ppermute(lax.slice_in_dim(block, block.shape[dim] - width, None, axis...]
    all_gather x0 -> x1, blocking collectives: none -> 16.9 us  [local(): block_grad = jnp.sum(lax.all_gather(own_rows, 'lat'), axis=0)]
    ppermute x10, waiting for transfers between devices: 30.8 us -> 41.3 us  [swapped(): return lax.ppermute(value, axis, pairs)]
    ppermute x5, waiting for transfers between devices: 0.01 us -> 10.1 us  [extended(): lax.ppermute(lax.slice_in_dim(block, 0, width, axis=dim), axis, backward)]
    ppermute x10, starting transfers between devices: 46.8 us -> 54.1 us  [swapped(): return lax.ppermute(value, axis, pairs)]
    ppermute x5, waiting for transfers between devices: 5.53 us -> 12.1 us  [extended(): lax.ppermute(lax.slice_in_dim(block, block.shape[dim] - width, None, axis...]
    psum x1, blocking collectives: 102 us -> 95.9 us  [local(): log_amp, embed_grad = lax.psum((amp_part, contrib), ('state', 'lat'))]
  transfers between devices with their start and end apart: 21 -> 20, of which waited for: 10 -> 12; matrix products, arithmetic and copies ran while one was open for 9% -> 6% of each run, Pallas kernels for 0% -> 0%
where the time goes in v1:
time: 333 us; the launch traced here: 331 us
  blocking collectives  113 us (34%)
  starting transfers between devices  101 us (30%)
  waiting for transfers between devices  63.5 us (19%)
  other arithmetic  21.6 us (6%)
  local copies, waits for them, and re-layouts  18.6 us (6%)
  matrix products  12.9 us (4%)
    psum x1, blocking collectives, local(): log_amp, embed_grad = lax.psum((amp_part, contrib), ('state', 'lat'))  95.9 us
    ppermute x10, starting transfers between devices, swapped(): return lax.ppermute(value, axis, pairs)  54.1 us
    ppermute x10, waiting for transfers between devices, swapped(): return lax.ppermute(value, axis, pairs)  41.3 us
    ppermute x5, starting transfers between devices, extended(): lax.ppermute(lax.slice_in_dim(block, 0, width, axis=dim), axis, backward)  35.4 us
    all_gather x1, blocking collectives, local(): block_grad = jnp.sum(lax.all_gather(own_rows, 'lat'), axis=0)  16.9 us
    ppermute x5, waiting for transfers between devices, extended(): lax.ppermute(lax.slice_in_dim(block, block.shape[dim] - width, None, axis...  12.1 us
    unnamed x22, other arithmetic  11.9 us
    ppermute x5, starting transfers between devices, extended(): lax.ppermute(lax.slice_in_dim(block, block.shape[dim] - width, None, axis...  11 us
  transfers between devices with their start and end apart: 20, of which 12 were waited for; matrix products, arithmetic and copies ran while one was open for 6% of the time, Pallas kernels for 0%

profile of v1, /device:TPU:1, one launch (start us, length us, event | category | flops | bytes accessed | tf_op | source)
XLA Modules:
  0.0 331.5 jit_solution(3775132777399737404)
XLA Ops:
  1.5 8.8 %collective-permute-start.1 = (bf16[1,1,1,128]{3,2,1,0:T(2,128)(2,1)S(1)}, bf16[1,1,1,128]{3,2,1,0:T(2,128)(2,1)S(1)}, u32[]{:S(2)}, u32[]{:S(2)}) collective-permute-start(bf16[1,1,1,128]{3,2,1,0:T(2,128)(2,1)S(1)} %convert_bitcast_fusion), channel_id=1, source_target_pairs={{1,0},{2,1},{3,2},{4,3},{5,4},{6,5},{7,6},{0,7},{9,8},{10,9},{11,1... | collective-permute-start | bytes 776 | tf_op jit(solution)/shard_map/ppermute | solution.py:17
  10.2 1.9 collective-permute-start
  12.2 1.1 collective-permute-done
  18.8 5.6 %collective-permute-start.3 = (bf16[1,64,1,128]{3,1,2,0:T(8,128)(2,1)S(1)}, bf16[1,64,1,128]{3,1,2,0:T(8,128)(2,1)S(1)}, u32[]{:S(2)}, u32[]{:S(2)}) collective-permute-start(bf16[1,64,1,128]{3,1,2,0:T(8,128)(2,1)S(1)} %fusion.29), channel_id=1, source_target_pairs={{1,0},{2,1},{3,2},{4,3},{5,4},{6,5},{7,6},{0,7},{9,8},{10,9},{11,1... | collective-permute-start | bytes 49160 | tf_op jit(solution)/shard_map/ppermute | solution.py:17
  24.3 1.9 collective-permute-start.2
  26.3 1.1 collective-permute-done.2
  27.6 1.9 collective-permute-start.4
  29.6 3.4 %collective-permute-done.4 = bf16[1,64,3,130]{3,1,2,0:T(8,128)(2,1)S(1)} collective-permute-done((bf16[1,64,3,130]{3,1,2,0:T(8,128)(2,1)S(1)}, bf16[1,64,3,130]{3,1,2,0:T(8,128)(2,1)S(1)}, u32[]{:S(2)}, u32[]{:S(2)}) %collective-permute-start.4) | collective-permute-done | bytes 49952 | tf_op jit(solution)/shard_map/ppermute | solution.py:25
  33.1 4.1 %collective-permute-start.5 = (bf16[2,64,3,130]{3,1,2,0:T(8,128)(2,1)S(1)}, bf16[2,64,3,130]{3,1,2,0:T(8,128)(2,1)}, u32[]{:S(2)}, u32[]{:S(2)}) collective-permute-start(bf16[2,64,3,130]{3,1,2,0:T(8,128)(2,1)S(1)} %maximum_select_fusion.3), channel_id=1, source_target_pairs={{0,64},{8,72},{16,80},{24,88},{32,96},{40,104},{48,112},{56,120},{... | collective-permute-start | bytes 299528 | tf_op jit(solution)/shard_map/ppermute | solution.py:25
  38.4 4.3 %collective-permute-done.5 = bf16[2,64,3,130]{3,1,2,0:T(8,128)(2,1)} collective-permute-done((bf16[2,64,3,130]{3,1,2,0:T(8,128)(2,1)S(1)}, bf16[2,64,3,130]{3,1,2,0:T(8,128)(2,1)}, u32[]{:S(2)}, u32[]{:S(2)}) %collective-permute-start.5) | collective-permute-done | bytes 99872 | tf_op jit(solution)/shard_map/ppermute | solution.py:25
  42.7 1.2 maximum_select_fusion.2
  43.8 8.3 %collective-permute-start.6 = (bf16[4,64,3,130]{3,1,2,0:T(8,128)(2,1)S(1)}, bf16[4,64,3,130]{3,1,2,0:T(8,128)(2,1)S(1)}, u32[]{:S(2)}, u32[]{:S(2)}) collective-permute-start(bf16[4,64,3,130]{3,1,2,0:T(8,128)(2,1)S(1)} %maximum_select_fusion.2), channel_id=1, source_target_pairs={{0,128},{8,136},{16,144},{24,152},{32,160},{40,168},{48,176},{56,1... | collective-permute-start | bytes 599048 | tf_op jit(solution)/shard_map/ppermute | solution.py:25
  52.2 7.4 %collective-permute-done.6 = bf16[4,64,3,130]{3,1,2,0:T(8,128)(2,1)S(1)} collective-permute-done((bf16[4,64,3,130]{3,1,2,0:T(8,128)(2,1)S(1)}, bf16[4,64,3,130]{3,1,2,0:T(8,128)(2,1)S(1)}, u32[]{:S(2)}, u32[]{:S(2)}) %collective-permute-start.6) | collective-permute-done | bytes 199712 | tf_op jit(solution)/shard_map/ppermute | solution.py:25
  59.9 4.8 %collective-permute-start.7 = (bf16[8,64,3,130]{3,1,2,0:T(8,128)(2,1)S(1)}, bf16[8,64,3,130]{3,1,2,0:T(8,128)(2,1)S(1)}, u32[]{:S(2)}, u32[]{:S(2)}) collective-permute-start(bf16[8,64,3,130]{3,1,2,0:T(8,128)(2,1)S(1)} %maximum_select_fusion.1), channel_id=1, source_target_pairs={{0,256},{8,264},{16,272},{24,280},{32,288},{40,296},{48,304},{56,3... | collective-permute-start | bytes 1198088 | tf_op jit(solution)/shard_map/ppermute | solution.py:25
  65.4 12.0 %collective-permute-done.7 = bf16[8,64,3,130]{3,1,2,0:T(8,128)(2,1)S(1)} collective-permute-done((bf16[8,64,3,130]{3,1,2,0:T(8,128)(2,1)S(1)}, bf16[8,64,3,130]{3,1,2,0:T(8,128)(2,1)S(1)}, u32[]{:S(2)}, u32[]{:S(2)}) %collective-permute-start.7) | collective-permute-done | bytes 399392 | tf_op jit(solution)/shard_map/ppermute | solution.py:25
  79.6 1.4 multiply_convert_fusion
  80.9 10.2 %collective-permute-start.9 = (bf16[16,64,1,128]{3,1,2,0:T(8,128)(2,1)S(1)}, bf16[16,64,1,128]{3,1,2,0:T(8,128)(2,1)S(1)}, u32[]{:S(2)}, u32[]{:S(2)}) collective-permute-start(bf16[16,64,1,128]{3,1,2,0:T(8,128)(2,1)S(1)} %get-tuple-element.37), channel_id=1, source_target_pairs={{1,0},{2,1},{3,2},{4,3},{5,4},{6,5},{7,6},{0,7},{9,8},{10,9},{11,1... | collective-permute-start | bytes 786440 | tf_op jit(solution)/shard_map/ppermute | solution.py:17
  91.2 1.9 collective-permute-start.8
  93.9 10.1 %collective-permute-done.9 = bf16[16,64,1,128]{3,1,2,0:T(8,128)(2,1)S(1)} collective-permute-done((bf16[16,64,1,128]{3,1,2,0:T(8,128)(2,1)S(1)}, bf16[16,64,1,128]{3,1,2,0:T(8,128)(2,1)S(1)}, u32[]{:S(2)}, u32[]{:S(2)}) %collective-permute-start.9) | collective-permute-done | bytes 262176 | tf_op jit(solution)/shard_map/ppermute | solution.py:17
  104.0 9.2 %collective-permute-done.8 = bf16[16,64,1,128]{3,1,2,0:T(8,128)(2,1)S(1)} collective-permute-done((bf16[16,64,1,128]{3,1,2,0:T(8,128)(2,1)S(1)}, bf16[16,64,1,128]{3,1,2,0:T(8,128)(2,1)S(1)}, u32[]{:S(2)}, u32[]{:S(2)}) %collective-permute-start.8) | collective-permute-done | bytes 262176 | tf_op jit(solution)/shard_map/ppermute | solution.py:14
  115.1 2.0 fusion.67
  117.2 8.5 %collective-permute-start.11 = (bf16[16,64,1,128]{3,1,2,0:T(8,128)(2,1)S(1)}, bf16[16,64,1,128]{3,1,2,0:T(8,128)(2,1)S(1)}, u32[]{:S(2)}, u32[]{:S(2)}) collective-permute-start(bf16[16,64,1,128]{3,1,2,0:T(8,128)(2,1)S(1)} %get-tuple-element.23), channel_id=1, source_target_pairs={{1,0},{2,1},{3,2},{4,3},{5,4},{6,5},{7,6},{0,7},{9,8},{10,9},{11,1... | collective-permute-start | bytes 786440 | tf_op jit(solution)/shard_map/ppermute | solution.py:17
  125.6 1.9 collective-permute-start.10
  128.1 1.2 mul.120
  129.3 1.3 mul.121
  131.4 1.0 copy.56
  134.0 1.3 mul.119
  135.3 1.2 mul.122
  137.9 1.1 maximum_dynamic-update-slice_fusion.7
  140.0 1.2 maximum_dynamic-update-slice_fusion.6
  143.6 2.4 collective-permute-start.13
  146.0 3.3 %collective-permute-start.12 = (bf16[16,64,1,128]{3,1,2,0:T(8,128)(2,1)S(1)}, bf16[16,64,1,128]{3,1,2,0:T(8,128)(2,1)}, u32[]{:S(2)}, u32[]{:S(2)}) collective-permute-start(bf16[16,64,1,128]{3,1,2,0:T(8,128)(2,1)S(1)} %fusion.26), channel_id=1, source_target_pairs={{0,1},{1,2},{2,3},{3,4},{4,5},{5,6},{6,7},{7,0},{8,9},{9,10},{10,1... | collective-permute-start | bytes 786440 | tf_op jit(solution)/shard_map/ppermute | solution.py:14
  150.9 1.8 copy.50
  152.7 1.8 copy.52
  156.6 1.1 maximum_dynamic-update-slice_fusion.3
  158.7 1.2 maximum_dynamic-update-slice_fusion.2
  161.1 2.4 convolution_bitcast_fusion.1
  163.9 4.6 %collective-permute-start.14 = (f32[32,1,2,576]{3,0,2,1:T(8,128)S(1)}, f32[32,1,2,576]{3,0,2,1:T(8,128)S(1)}, u32[]{:S(2)}, u32[]{:S(2)}) collective-permute-start(f32[32,1,2,576]{3,0,2,1:T(8,128)S(1)} %slice_select_fusion.1), channel_id=1, source_target_pairs={{0,16},{8,24},{16,0},{24,8},{32,48},{40,56},{48,32},{56,40},{64,80... | collective-permute-start | bytes 442376 | tf_op jit(solution)/shard_map/ppermute | solution.py:25
  168.6 2.6 fusion.20
  171.2 4.1 %collective-permute-start.16 = (f32[8,64,1,128]{3,1,2,0:T(8,128)S(1)}, f32[8,64,1,128]{3,1,2,0:T(8,128)S(1)}, u32[]{:S(2)}, u32[]{:S(2)}) collective-permute-start(f32[8,64,1,128]{3,1,2,0:T(8,128)S(1)} %slice_select_fusion), channel_id=1, source_target_pairs={{0,256},{8,264},{16,272},{24,280},{32,288},{40,296},{48,304},{56,3... | collective-permute-start | bytes 786440 | tf_op jit(solution)/shard_map/ppermute | solution.py:25
  175.6 12.3 %collective-permute-done.16 = f32[8,64,1,128]{3,1,2,0:T(8,128)S(1)} collective-permute-done((f32[8,64,1,128]{3,1,2,0:T(8,128)S(1)}, f32[8,64,1,128]{3,1,2,0:T(8,128)S(1)}, u32[]{:S(2)}, u32[]{:S(2)}) %collective-permute-start.16) | collective-permute-done | bytes 262176 | tf_op jit(solution)/shard_map/ppermute | solution.py:25
  188.0 7.0 %collective-permute-start.17 = (f32[4,64,1,128]{3,1,2,0:T(8,128)S(1)}, f32[4,64,1,128]{3,1,2,0:T(8,128)S(1)}, u32[]{:S(2)}, u32[]{:S(2)}) collective-permute-start(f32[4,64,1,128]{3,1,2,0:T(8,128)S(1)} %slice_select_fusion.2), channel_id=1, source_target_pairs={{0,128},{8,136},{16,144},{24,152},{32,160},{40,168},{48,176},{56,1... | collective-permute-start | bytes 393224 | tf_op jit(solution)/shard_map/ppermute | solution.py:25
  195.0 2.2 collective-permute-start.15
  197.6 11.2 %collective-permute-start.18 = (f32[2,64,1,128]{3,1,2,0:T(8,128)S(1)}, f32[2,64,1,128]{3,1,2,0:T(8,128)S(1)}, u32[]{:S(2)}, u32[]{:S(2)}) collective-permute-start(f32[2,64,1,128]{3,1,2,0:T(8,128)S(1)} %slice_select_fusion.4), channel_id=1, source_target_pairs={{0,64},{8,72},{16,80},{24,88},{32,96},{40,104},{48,112},{56,120},{... | collective-permute-start | bytes 196616 | tf_op jit(solution)/shard_map/ppermute | solution.py:25
  208.9 1.6 collective-permute-done.18
  210.5 5.8 %collective-permute-start.19 = (f32[1,64,1,128]{3,1,2,0:T(8,128)S(1)}, f32[1,64,1,128]{3,1,2,0:T(8,128)S(1)}, u32[]{:S(2)}, u32[]{:S(2)}) collective-permute-start(f32[1,64,1,128]{3,1,2,0:T(8,128)S(1)} %slice_select_fusion.5), channel_id=1, source_target_pairs={{0,32},{8,40},{16,48},{24,56},{32,0},{40,8},{48,16},{56,24},{64,96... | collective-permute-start | bytes 98312 | tf_op jit(solution)/shard_map/ppermute | solution.py:25
  216.3 16.9 %all-gather = f32[128,1,2,576]{3,2,1,0:T(2,128)S(1)} all-gather(f32[16,1,2,576]{3,2,1,0:T(2,128)S(1)} %copy.53), channel_id=2, replica_groups=mesh['state'=64,'lat'=8] {'lat'}, dimensions={0}, use_global_device_ids=true | all-gather | bytes 663552 | tf_op jit(solution)/shard_map/all_gather | solution.py:192
  235.6 95.9 %all-reduce = (f32[16,64]{1,0:T(8,128)}, f32[64,9]{0,1:T(8,128)}) all-reduce(f32[16,64]{1,0:T(8,128)S(1)} %broadcast_multiply_fusion.1, f32[64,9]{0,1:T(8,128)S(1)} %stack.47), channel_id=1, replica_groups=mesh['state'=64,'lat'=8] {'state','lat'}, use_global_device_ids=true, to_apply=%region_1.2 | all-reduce | flops 1600 | bytes 12800 | tf_op jit(solution)/shard_map/psum | solution.py:189
  (160 shorter events, 30.2 us)
Async XLA Ops:
  0.6 28.9 %copy-start = (bf16[16,1,2,64,576]{4,3,2,1,0:T(8,128)(2,1)S(1)}, bf16[16,1,2,64,576]{4,3,2,1,0:T(8,128)(2,1)}, u32[]{:S(2)}) copy-start(bf16[16,1,2,64,576]{4,3,2,1,0:T(8,128)(2,1)} %param.7) | copy-start | bytes 7077892
  1.5 10.7 %collective-permute-start.1 = (bf16[1,1,1,128]{3,2,1,0:T(2,128)(2,1)S(1)}, bf16[1,1,1,128]{3,2,1,0:T(2,128)(2,1)S(1)}, u32[]{:S(2)}, u32[]{:S(2)}) collective-permute-start(bf16[1,1,1,128]{3,2,1,0:T(2,128)(2,1)S(1)} %convert_bitcast_fusion), channel_id=1, source_target_pairs={{1,0},{2,1},{3,2},{4,3},{5,4},{6,5},{7,6},{0,7},{9,8},{10,9},{11,1... | collective-permute-start | bytes 776 | tf_op jit(solution)/shard_map/ppermute | solution.py:17
  10.2 3.0 collective-permute-start
  12.2 6.6 %copy-start.4 = (bf16[1,1,1,128]{3,2,1,0:T(2,128)(2,1)}, bf16[1,1,1,128]{3,2,1,0:T(2,128)(2,1)S(1)}, u32[]{:S(2)}) copy-start(bf16[1,1,1,128]{3,2,1,0:T(2,128)(2,1)S(1)} %collective-permute-done.1) | copy-start | bytes 772
  13.3 11.1 %copy-start.6 = (bf16[1,1,1,128]{3,2,1,0:T(2,128)(2,1)}, bf16[1,1,1,128]{3,2,1,0:T(2,128)(2,1)S(1)}, u32[]{:S(2)}) copy-start(bf16[1,1,1,128]{3,2,1,0:T(2,128)(2,1)S(1)} %collective-permute-done) | copy-start | bytes 772
  18.8 7.5 %collective-permute-start.3 = (bf16[1,64,1,128]{3,1,2,0:T(8,128)(2,1)S(1)}, bf16[1,64,1,128]{3,1,2,0:T(8,128)(2,1)S(1)}, u32[]{:S(2)}, u32[]{:S(2)}) collective-permute-start(bf16[1,64,1,128]{3,1,2,0:T(8,128)(2,1)S(1)} %fusion.29), channel_id=1, source_target_pairs={{1,0},{2,1},{3,2},{4,3},{5,4},{6,5},{7,6},{0,7},{9,8},{10,9},{11,1... | collective-permute-start | bytes 49160 | tf_op jit(solution)/shard_map/ppermute | solution.py:17
  24.3 3.1 collective-permute-start.2
  27.6 5.4 %collective-permute-start.4 = (bf16[1,64,3,130]{3,1,2,0:T(8,128)(2,1)S(1)}, bf16[1,64,3,130]{3,1,2,0:T(8,128)(2,1)S(1)}, u32[]{:S(2)}, u32[]{:S(2)}) collective-permute-start(bf16[1,64,3,130]{3,1,2,0:T(8,128)(2,1)S(1)} %pad_maximum_fusion.21), channel_id=1, source_target_pairs={{0,32},{8,40},{16,48},{24,56},{32,0},{40,8},{48,16},{56,24},{64,96... | collective-permute-start | bytes 149768 | tf_op jit(solution)/shard_map/ppermute | solution.py:25
  33.1 9.5 %collective-permute-start.5 = (bf16[2,64,3,130]{3,1,2,0:T(8,128)(2,1)S(1)}, bf16[2,64,3,130]{3,1,2,0:T(8,128)(2,1)}, u32[]{:S(2)}, u32[]{:S(2)}) collective-permute-start(bf16[2,64,3,130]{3,1,2,0:T(8,128)(2,1)S(1)} %maximum_select_fusion.3), channel_id=1, source_target_pairs={{0,64},{8,72},{16,80},{24,88},{32,96},{40,104},{48,112},{56,120},{... | collective-permute-start | bytes 299528 | tf_op jit(solution)/shard_map/ppermute | solution.py:25
  43.8 15.8 %collective-permute-start.6 = (bf16[4,64,3,130]{3,1,2,0:T(8,128)(2,1)S(1)}, bf16[4,64,3,130]{3,1,2,0:T(8,128)(2,1)S(1)}, u32[]{:S(2)}, u32[]{:S(2)}) collective-permute-start(bf16[4,64,3,130]{3,1,2,0:T(8,128)(2,1)S(1)} %maximum_select_fusion.2), channel_id=1, source_target_pairs={{0,128},{8,136},{16,144},{24,152},{32,160},{40,168},{48,176},{56,1... | collective-permute-start | bytes 599048 | tf_op jit(solution)/shard_map/ppermute | solution.py:25
  52.2 25.9 %copy-start.17 = (f32[4]{0:T(128)}, f32[4]{0:T(128)S(1)}, u32[]{:S(2)}) copy-start(f32[4]{0:T(128)S(1)} %compare_convert_fusion) | copy-start | bytes 52
  59.9 17.6 %collective-permute-start.7 = (bf16[8,64,3,130]{3,1,2,0:T(8,128)(2,1)S(1)}, bf16[8,64,3,130]{3,1,2,0:T(8,128)(2,1)S(1)}, u32[]{:S(2)}, u32[]{:S(2)}) collective-permute-start(bf16[8,64,3,130]{3,1,2,0:T(8,128)(2,1)S(1)} %maximum_select_fusion.1), channel_id=1, source_target_pairs={{0,256},{8,264},{16,272},{24,280},{32,288},{40,296},{48,304},{56,3... | collective-permute-start | bytes 1198088 | tf_op jit(solution)/shard_map/ppermute | solution.py:25
  78.1 37.1 %copy-start.1 = (bf16[16,64,3,130]{3,1,2,0:T(8,128)(2,1)}, bf16[16,64,3,130]{3,1,2,0:T(8,128)(2,1)S(1)}, u32[]{:S(2)}) copy-start(bf16[16,64,3,130]{3,1,2,0:T(8,128)(2,1)S(1)} %maximum_select_fusion) | copy-start | bytes 2396164
  80.9 23.0 %collective-permute-start.9 = (bf16[16,64,1,128]{3,1,2,0:T(8,128)(2,1)S(1)}, bf16[16,64,1,128]{3,1,2,0:T(8,128)(2,1)S(1)}, u32[]{:S(2)}, u32[]{:S(2)}) collective-permute-start(bf16[16,64,1,128]{3,1,2,0:T(8,128)(2,1)S(1)} %get-tuple-element.37), channel_id=1, source_target_pairs={{1,0},{2,1},{3,2},{4,3},{5,4},{6,5},{7,6},{0,7},{9,8},{10,9},{11,1... | collective-permute-start | bytes 786440 | tf_op jit(solution)/shard_map/ppermute | solution.py:17
  91.2 22.0 %collective-permute-start.8 = (bf16[16,64,1,128]{3,1,2,0:T(8,128)(2,1)S(1)}, bf16[16,64,1,128]{3,1,2,0:T(8,128)(2,1)S(1)}, u32[]{:S(2)}, u32[]{:S(2)}) collective-permute-start(bf16[16,64,1,128]{3,1,2,0:T(8,128)(2,1)S(1)} %get-tuple-element.37), channel_id=1, source_target_pairs={{0,1},{1,2},{2,3},{3,4},{4,5},{5,6},{6,7},{7,0},{8,9},{9,10},{10,1... | collective-permute-start | bytes 786440 | tf_op jit(solution)/shard_map/ppermute | solution.py:14
  93.9 21.3 %copy-start.9 = (f32[16,64]{1,0:T(8,128)}, f32[16,64]{1,0:T(8,128)S(1)}, u32[]{:S(2)}) copy-start(f32[16,64]{1,0:T(8,128)S(1)} %broadcast_multiply_fusion) | copy-start | bytes 12292
  117.2 19.3 %collective-permute-start.11 = (bf16[16,64,1,128]{3,1,2,0:T(8,128)(2,1)S(1)}, bf16[16,64,1,128]{3,1,2,0:T(8,128)(2,1)S(1)}, u32[]{:S(2)}, u32[]{:S(2)}) collective-permute-start(bf16[16,64,1,128]{3,1,2,0:T(8,128)(2,1)S(1)} %get-tuple-element.23), channel_id=1, source_target_pairs={{1,0},{2,1},{3,2},{4,3},{5,4},{6,5},{7,6},{0,7},{9,8},{10,9},{11,1... | collective-permute-start | bytes 786440 | tf_op jit(solution)/shard_map/ppermute | solution.py:17
  125.6 10.9 %collective-permute-start.10 = (bf16[16,64,1,128]{3,1,2,0:T(8,128)(2,1)S(1)}, bf16[16,64,1,128]{3,1,2,0:T(8,128)(2,1)}, u32[]{:S(2)}, u32[]{:S(2)}) collective-permute-start(bf16[16,64,1,128]{3,1,2,0:T(8,128)(2,1)S(1)} %get-tuple-element.23), channel_id=1, source_target_pairs={{0,1},{1,2},{2,3},{3,4},{4,5},{5,6},{6,7},{7,0},{8,9},{9,10},{10,1... | collective-permute-start | bytes 786440 | tf_op jit(solution)/shard_map/ppermute | solution.py:14
  141.8 0.9 copy-start.3
  141.8 1.1 copy-start.21
  143.6 10.9 %collective-permute-start.13 = (bf16[16,64,1,128]{3,1,2,0:T(8,128)(2,1)S(1)}, bf16[16,64,1,128]{3,1,2,0:T(8,128)(2,1)S(1)}, u32[]{:S(2)}, u32[]{:S(2)}) collective-permute-start(bf16[16,64,1,128]{3,1,2,0:T(8,128)(2,1)S(1)} %fusion.26), channel_id=1, source_target_pairs={{1,0},{2,1},{3,2},{4,3},{5,4},{6,5},{7,6},{0,7},{9,8},{10,9},{11,1... | collective-permute-start | bytes 786440 | tf_op jit(solution)/shard_map/ppermute | solution.py:17
  146.0 9.2 %collective-permute-start.12 = (bf16[16,64,1,128]{3,1,2,0:T(8,128)(2,1)S(1)}, bf16[16,64,1,128]{3,1,2,0:T(8,128)(2,1)}, u32[]{:S(2)}, u32[]{:S(2)}) collective-permute-start(bf16[16,64,1,128]{3,1,2,0:T(8,128)(2,1)S(1)} %fusion.26), channel_id=1, source_target_pairs={{0,1},{1,2},{2,3},{3,4},{4,5},{5,6},{6,7},{7,0},{8,9},{9,10},{10,1... | collective-permute-start | bytes 786440 | tf_op jit(solution)/shard_map/ppermute | solution.py:14
  161.1 2.5 copy-start.8
  161.1 2.8 copy-start.2
  161.1 7.5 %copy-start.10 = (f32[16,64]{1,0:T(8,128)S(1)}, f32[16,64]{1,0:T(8,128)}, u32[]{:S(2)}) copy-start(f32[16,64]{1,0:T(8,128)} %copy-done.9) | copy-start | bytes 12292
  163.9 11.5 %collective-permute-start.14 = (f32[32,1,2,576]{3,0,2,1:T(8,128)S(1)}, f32[32,1,2,576]{3,0,2,1:T(8,128)S(1)}, u32[]{:S(2)}, u32[]{:S(2)}) collective-permute-start(f32[32,1,2,576]{3,0,2,1:T(8,128)S(1)} %slice_select_fusion.1), channel_id=1, source_target_pairs={{0,16},{8,24},{16,0},{24,8},{32,48},{40,56},{48,32},{56,40},{64,80... | collective-permute-start | bytes 442376 | tf_op jit(solution)/shard_map/ppermute | solution.py:25
  168.6 6.8 %copy-start.19 = (f32[16]{0:T(128)S(1)}, f32[16]{0:T(128)}, u32[]{:S(2)}) copy-start(f32[16]{0:T(128)} %compare_convert_fusion.1) | copy-start | bytes 196
  168.6 6.8 %copy-start.20 = (f32[64]{0:T(128)S(1)}, f32[64]{0:T(128)}, u32[]{:S(2)}) copy-start(f32[64]{0:T(128)} %mul.122) | copy-start | bytes 772
  171.2 16.6 %collective-permute-start.16 = (f32[8,64,1,128]{3,1,2,0:T(8,128)S(1)}, f32[8,64,1,128]{3,1,2,0:T(8,128)S(1)}, u32[]{:S(2)}, u32[]{:S(2)}) collective-permute-start(f32[8,64,1,128]{3,1,2,0:T(8,128)S(1)} %slice_select_fusion), channel_id=1, source_target_pairs={{0,256},{8,264},{16,272},{24,280},{32,288},{40,296},{48,304},{56,3... | collective-permute-start | bytes 786440 | tf_op jit(solution)/shard_map/ppermute | solution.py:25
  175.5 58.6 %copy-start.18 = (s32[1,1,128]{2,1,0:T(1,128)S(1)}, s32[1,1,128]{2,1,0:T(1,128)}, u32[]{:S(2)}) copy-start(s32[1,1,128]{2,1,0:T(1,128)} %param.5) | copy-start | bytes 1540
  175.5 58.7 %copy-start.12 = (bf16[1,1,1,128]{3,2,1,0:T(2,128)(2,1)S(1)}, bf16[1,1,1,128]{3,2,1,0:T(2,128)(2,1)}, u32[]{:S(2)}) copy-start(bf16[1,1,1,128]{3,2,1,0:T(2,128)(2,1)} %get-tuple-element.20) | copy-start | bytes 772
  175.5 58.9 %copy-start.13 = (bf16[1,1,1,128]{3,2,1,0:T(2,128)(2,1)S(1)}, bf16[1,1,1,128]{3,2,1,0:T(2,128)(2,1)}, u32[]{:S(2)}) copy-start(bf16[1,1,1,128]{3,2,1,0:T(2,128)(2,1)} %get-tuple-element.18) | copy-start | bytes 772
  175.5 59.0 %copy-start.14 = (bf16[1,1,1,128]{3,2,1,0:T(2,128)(2,1)S(1)}, bf16[1,1,1,128]{3,2,1,0:T(2,128)(2,1)}, u32[]{:S(2)}) copy-start(bf16[1,1,1,128]{3,2,1,0:T(2,128)(2,1)} %get-tuple-element.16) | copy-start | bytes 772
  175.5 59.2 %copy-start.15 = (bf16[1,1,1,128]{3,2,1,0:T(2,128)(2,1)S(1)}, bf16[1,1,1,128]{3,2,1,0:T(2,128)(2,1)}, u32[]{:S(2)}) copy-start(bf16[1,1,1,128]{3,2,1,0:T(2,128)(2,1)} %get-tuple-element.14) | copy-start | bytes 772
  175.6 59.3 %copy-start.16 = (bf16[1,1,1,128]{3,2,1,0:T(2,128)(2,1)S(1)}, bf16[1,1,1,128]{3,2,1,0:T(2,128)(2,1)}, u32[]{:S(2)}) copy-start(bf16[1,1,1,128]{3,2,1,0:T(2,128)(2,1)} %get-tuple-element.12) | copy-start | bytes 772
  175.6 59.5 %copy-start.11 = (bf16[1,1,1,128]{3,2,1,0:T(2,128)(2,1)S(1)}, bf16[1,1,1,128]{3,2,1,0:T(2,128)(2,1)}, u32[]{:S(2)}) copy-start(bf16[1,1,1,128]{3,2,1,0:T(2,128)(2,1)} %get-tuple-element.22) | copy-start | bytes 772
  175.6 59.6 %copy-start.7 = (bf16[1,1,1,128]{3,2,1,0:T(2,128)(2,1)S(1)}, bf16[1,1,1,128]{3,2,1,0:T(2,128)(2,1)}, u32[]{:S(2)}) copy-start(bf16[1,1,1,128]{3,2,1,0:T(2,128)(2,1)} %copy-done.6) | copy-start | bytes 772
  175.6 59.8 %copy-start.5 = (bf16[1,1,1,128]{3,2,1,0:T(2,128)(2,1)S(1)}, bf16[1,1,1,128]{3,2,1,0:T(2,128)(2,1)}, u32[]{:S(2)}) copy-start(bf16[1,1,1,128]{3,2,1,0:T(2,128)(2,1)} %copy-done.4) | copy-start | bytes 772
  188.0 9.6 %collective-permute-start.17 = (f32[4,64,1,128]{3,1,2,0:T(8,128)S(1)}, f32[4,64,1,128]{3,1,2,0:T(8,128)S(1)}, u32[]{:S(2)}, u32[]{:S(2)}) collective-permute-start(f32[4,64,1,128]{3,1,2,0:T(8,128)S(1)} %slice_select_fusion.2), channel_id=1, source_target_pairs={{0,128},{8,136},{16,144},{24,152},{32,160},{40,168},{48,176},{56,1... | collective-permute-start | bytes 393224 | tf_op jit(solution)/shard_map/ppermute | solution.py:25
  195.0 13.8 %collective-permute-start.15 = (f32[16,1,2,576]{3,0,2,1:T(8,128)S(1)}, f32[16,1,2,576]{3,0,2,1:T(8,128)S(1)}, u32[]{:S(2)}, u32[]{:S(2)}) collective-permute-start(f32[16,1,2,576]{3,0,2,1:T(8,128)S(1)} %slice_select_fusion.3), channel_id=1, source_target_pairs={{0,8},{8,0},{16,24},{24,16},{32,40},{40,32},{48,56},{56,48},{64,72... | collective-permute-start | bytes 221192 | tf_op jit(solution)/shard_map/ppermute | solution.py:25
  197.6 12.9 %collective-permute-start.18 = (f32[2,64,1,128]{3,1,2,0:T(8,128)S(1)}, f32[2,64,1,128]{3,1,2,0:T(8,128)S(1)}, u32[]{:S(2)}, u32[]{:S(2)}) collective-permute-start(f32[2,64,1,128]{3,1,2,0:T(8,128)S(1)} %slice_select_fusion.4), channel_id=1, source_target_pairs={{0,64},{8,72},{16,80},{24,88},{32,96},{40,104},{48,112},{56,120},{... | collective-permute-start | bytes 196616 | tf_op jit(solution)/shard_map/ppermute | solution.py:25
  210.5 23.6 %collective-permute-start.19 = (f32[1,64,1,128]{3,1,2,0:T(8,128)S(1)}, f32[1,64,1,128]{3,1,2,0:T(8,128)S(1)}, u32[]{:S(2)}, u32[]{:S(2)}) collective-permute-start(f32[1,64,1,128]{3,1,2,0:T(8,128)S(1)} %slice_select_fusion.5), channel_id=1, source_target_pairs={{0,32},{8,40},{16,48},{24,56},{32,0},{40,8},{48,16},{56,24},{64,96... | collective-permute-start | bytes 98312 | tf_op jit(solution)/shard_map/ppermute | solution.py:25
